TPU v7x, 32 devices: a whole 2x2x4 slice. The times are simulated.
32 devices in a mesh: dp: 8 (over z, y), tensor: 4 (over x, core).
Axes of the slice: x: 2, y: 2, z: 4, core: 2. Of those that a mesh axis runs over, the one named last changes fastest.
Arguments:
- query: bfloat16 [64, 64, 128], P('dp', 'tensor'), may hold values from -8 to 8
- kv_pages: bfloat16 [560, 8, 2, 128, 128], P('dp', 'tensor'), may hold values from -8 to 8
- move_plan: int32 [8, 3, 12], P('dp'), may hold values from 0 to 69, as said below
- move_count: int32 [8], P('dp'), may hold values from 9 to 12
- block_table: int32 [64, 8], P('dp'), may hold values from 0 to 69, as said below
- seq_lens: int32 [64], P('dp'), may hold values from 1 to 1024
- out_weight: bfloat16 [8192, 8192], P('tensor', 'dp'), may hold values from -0.0625 to 0.0625
Outputs:
- new_pages: bfloat16 [560, 8, 2, 128, 128], P('dp', 'tensor')
- projected: bfloat16 [64, 8192], P(None, 'dp')
Inputs may be any that keep to these rules, and one draw needn't show every extreme that they name: `move_plan`: row 0 holds the device's own source slots, distinct within a device; row 1 target devices; row 2 target slots. Entries at or past the device's move_count are padding to be ignored. At most 2 valid moves go from one device to one device, and some pair has exactly 2. The (target device, target slot) pairs of all valid moves are distinct. `block_table`: all entries of the sequences of one device are distinct slots of that device; sequence s belongs to device s // 8.
All inputs are finite; a program needn't handle non-finite values.
Results may differ from a plain program's by a relative error of at most 0.0055.
Values may be sent and summed in bfloat16 or wider, within the bound.
No kernel may reach another device: no remote copies, remote signals or barrier semaphores. Data moves between devices by JAX's collectives and lax.ppermute only.
A program may use at most 128 MiB of HBM per device.

v0:
```python
import math
import jax
import jax.numpy as jnp
from jax import lax
from jax.sharding import PartitionSpec as P

HD = 128
BLOCK = 128
BLOCKS = 8
CAP = 2


def body(query, kv_pages, move_plan, move_count, block_table, seq_lens, out_weight):
    slots_here = kv_pages.shape[0]
    move_total = move_plan.shape[2]
    devices = lax.axis_size("dp")
    capacity = CAP
    holding_rows = devices * capacity
    move_list = move_plan[0]
    move_index = jnp.arange(move_total, dtype=jnp.int32)
    is_valid = move_index < move_count[0]
    target_dev = move_list[1]
    earlier = (
        (target_dev[:, None] == target_dev[None, :])
        & is_valid[None, :]
        & (move_index[None, :] < move_index[:, None])
    )
    dest_rank = jnp.sum(earlier.astype(jnp.int32), axis=1)
    send_row = jnp.where(is_valid, target_dev * capacity + dest_rank, -1)
    flat_pages = kv_pages.reshape(slots_here, -1)
    picked = flat_pages[move_list[0]]
    select = jnp.arange(holding_rows, dtype=jnp.int32)[:, None] == send_row[None, :]
    outgoing = jnp.dot(
        select.astype(jnp.bfloat16), picked, preferred_element_type=jnp.float32
    ).astype(jnp.bfloat16)
    outgoing = outgoing.reshape((holding_rows,) + kv_pages.shape[1:])
    out_slots = jnp.sum(select.astype(jnp.int32) * (move_list[2][None, :] + 1), axis=1) - 1
    slot_tags = out_slots.astype(jnp.float32).astype(jnp.bfloat16)
    arrived, arrived_tags = (
        lax.all_to_all(outgoing, "dp", split_axis=0, concat_axis=0, tiled=True),
        lax.all_to_all(slot_tags, "dp", split_axis=0, concat_axis=0, tiled=True),
    )
    incoming = arrived_tags.astype(jnp.float32).astype(jnp.int32)
    hit_table = jnp.arange(slots_here, dtype=jnp.int32)[:, None] == incoming[None, :]
    placed = jnp.dot(
        hit_table.astype(jnp.bfloat16),
        arrived.reshape(holding_rows, -1),
        preferred_element_type=jnp.float32,
    ).astype(jnp.bfloat16)
    written = jnp.any(hit_table, axis=1)
    new_pages = jnp.where(written[:, None], placed, flat_pages).reshape(kv_pages.shape)
    seq_here = query.shape[0]
    local_heads = new_pages.shape[1]
    head_dim = query.shape[2]
    group_size = query.shape[1] // local_heads
    context = BLOCKS * BLOCK
    gathered = new_pages[block_table]
    key_rows = jnp.transpose(gathered[:, :, :, 0], (0, 2, 1, 3, 4)).reshape(
        seq_here, local_heads, context, head_dim
    )
    value_rows = jnp.transpose(gathered[:, :, :, 1], (0, 2, 1, 3, 4)).reshape(
        seq_here, local_heads, context, head_dim
    )
    grouped = query.reshape(seq_here, local_heads, group_size, head_dim)
    score_scale = 1.0 / math.sqrt(HD)
    scores = (
        jnp.einsum("skgd,sktd->skgt", grouped, key_rows, preferred_element_type=jnp.float32)
        * score_scale
    )
    position = jnp.arange(context, dtype=jnp.int32)
    scores = jnp.where(position[None, None, None, :] < seq_lens[:, None, None, None], scores, -1e30)
    largest = jnp.max(scores, axis=-1, keepdims=True)
    expo = jnp.exp(scores - largest)
    weights = (expo / jnp.sum(expo, axis=-1, keepdims=True)).astype(jnp.bfloat16)
    mixed_heads = jnp.einsum(
        "skgt,sktd->skgd", weights, value_rows, preferred_element_type=jnp.float32
    )
    attention = mixed_heads.reshape(seq_here, local_heads * group_size * head_dim).astype(
        jnp.bfloat16
    )
    partial_sums = jnp.dot(
        lax.all_gather(attention, "dp", axis=0, tiled=True),
        out_weight,
        preferred_element_type=jnp.float32,
    )
    summed = lax.psum(partial_sums, "tensor")
    return (new_pages, summed.astype(jnp.bfloat16))


def solution(mesh):
    placed = (
        P("dp", "tensor", None),
        P("dp", "tensor", None, None, None),
        P("dp", None, None),
        P("dp"),
        P("dp", None),
        P("dp"),
        P("tensor", "dp"),
    )
    return jax.shard_map(
        body,
        mesh=mesh,
        in_specs=placed,
        out_specs=(P("dp", "tensor", None, None, None), P(None, "dp")),
        check_vma=False,
    )
```

profile of v0, /device:TPU:1, one launch (start us, length us, event | category | flops | bytes accessed | tf_op | source)
XLA Modules:
  0.0 194.9 jit_solution(8297206147046076033)
XLA Ops:
  0.6 0.0 copy-start
  0.6 0.7 slice_bitcast_fusion
  2.0 0.2 convert_reduce_fusion
  2.2 0.7 add_select_fusion
  2.8 0.1 select_reduce_fusion
  3.0 0.7 convert_element_type.79
  3.7 6.4 %all-to-all-start = ((bf16[8,2,1]{1,2,0:T(2,128)(2,1)}), bf16[8,2,1]{1,2,0:T(2,128)(2,1)S(1)}, u32[]{:S(2)}, u32[]{:S(2)}) async-start(bf16[8,2,1]{1,2,0:T(2,128)(2,1)} %convert_element_type.79), calls=%async_computation | async-start | bytes 8192 | tf_op jit(solution)/shard_map/all_to_all | solution.py:41
  10.0 0.7 fusion.16
  10.7 8.8 %pad.2 = bf16[72,512,128]{2,1,0:T(8,128)(2,1)} pad(bf16[70,512,128]{2,1,0:T(8,128)(2,1)} %bitcast.69, bf16[]{:T(256)} %constant.38), padding=0_2x0_0x0_0 | pad | bytes 18612226
  19.5 13.8 %copy.21 = bf16[9,8,512,128]{3,1,2,0:T(8,128)(2,1)} copy(bf16[9,8,512,128]{3,2,1,0:T(8,128)(2,1)} %bitcast.62) | data formatting | bytes 18874368
  33.3 7.8 %gather_fusion = bf16[12,65536]{1,0:T(8,128)(2,1)S(1)} fusion(bf16[70,65536]{1,0:T(8,128)(2,1)} %bitcast.59, s32[1024]{0:T(1024)S(1)} %pad_clamp_fusion.1), kind=kCustom, calls=%fused_computation | custom fusion | bytes 3145776 | tf_op jit(solution)/shard_map/gather | solution.py:31
  41.1 0.7 fusion.4
  41.8 1.9 copy.22
  43.7 5.4 %all-to-all-start.1 = ((bf16[16,2,2,128,128]{4,3,2,1,0:T(8,128)(2,1)}), bf16[16,2,2,128,128]{4,3,2,1,0:T(8,128)(2,1)S(1)}, u32[]{:S(2)}, u32[]{:S(2)}) async-start(bf16[16,2,2,128,128]{4,3,2,1,0:T(8,128)(2,1)} %bitcast.24), calls=%async_computation.1 | async-start | bytes 4194304 | tf_op jit(solution)/shard_map/all_to_all | solution.py:40
  49.2 0.1 reshape.158
  49.3 0.1 iota_compare_fusion
  49.4 0.1 convert_element_type.72
  49.4 0.1 fusion.12
  49.5 46.5 %all-to-all-done.1 = bf16[16,2,2,128,128]{4,3,2,1,0:T(8,128)(2,1)S(1)} async-done(((bf16[16,2,2,128,128]{4,3,2,1,0:T(8,128)(2,1)}), bf16[16,2,2,128,128]{4,3,2,1,0:T(8,128)(2,1)S(1)}, u32[]{:S(2)}, u32[]{:S(2)}) %all-to-all-start.1) | async-done | bytes 2097184 | tf_op jit(solution)/shard_map/all_to_all | solution.py:40
  96.0 10.8 %fusion.1 = bf16[70,65536]{1,0:T(8,128)(2,1)} fusion(bf16[70,65536]{1,0:T(8,128)(2,1)} %bitcast.60, pred[70]{0:T(512)(128)(4,1)S(1)} %fusion.12, bf16[2,8,512,128]{3,2,1,0:T(8,128)(2,1)S(1)} %bitcast.70, s32[16]{0:T(128)S(1)} %convert_element_type.72), kind=kOutput, calls=%fused_computation.4 | convolution fusion | flops 155976800 | bytes 20447366 | tf_op jit(solution)/shard_map/dot_general | solution.py:45
  106.8 9.9 %copy.24 = bf16[9,8,512,128]{3,2,1,0:T(8,128)(2,1)} copy(bf16[9,8,512,128]{3,1,2,0:T(8,128)(2,1)} %bitcast.61) | data formatting | bytes 18874368
  116.7 8.4 %slice.29 = bf16[70,512,128]{2,1,0:T(8,128)(2,1)} slice(bf16[72,512,128]{2,1,0:T(8,128)(2,1)} %bitcast.63), slice={[0:70], [0:512], [0:128]} | slice | bytes 18350080
  125.1 9.1 %gather_fusion.1 = bf16[64,2,2,128,128]{4,3,2,1,0:T(8,128)(2,1)} fusion(bf16[70,2,2,128,128]{4,3,2,1,0:T(8,128)(2,1)} %bitcast.64, s32[1024]{0:T(1024)S(1)} %pad_clamp_fusion), kind=kCustom, calls=%fused_computation.1 | custom fusion | bytes 16777472 | tf_op jit(solution)/shard_map/gather | solution.py:57
  134.2 3.8 %fusion.17 = (bf16[8,8,2,1,128,128]{5,4,3,2,1,0:T(8,128)(2,1)S(1)}, bf16[8,8,2,1,128,128]{5,4,3,2,1,0:T(8,128)(2,1)S(1)}) fusion(bf16[8,8,2,2,128,128]{5,4,3,2,1,0:T(8,128)(2,1)} %bitcast.66), kind=kLoop, calls=%fused_computation.41 | loop fusion | bytes 16777216 | tf_op jit(solution)/shard_map/slice | solution.py:58
  138.1 0.6 copy.19
  138.7 1.2 fusion.8
  139.8 0.3 fusion.18
  140.1 2.2 %copy.20 = bf16[8,8,2,1,128,128]{5,4,1,2,0,3:T(8,128)(2,1)} copy(bf16[8,8,2,1,128,128]{5,4,3,2,1,0:T(8,128)(2,1)S(1)} %get-tuple-element.3) | data formatting | bytes 8388608
  142.3 2.9 %fusion.9 = bf16[1,8,16,128]{3,2,1,0:T(8,128)(2,1)S(1)} fusion(bf16[8,2,1024,128]{3,2,1,0:T(8,128)(2,1)} %bitcast.67, f32[8,2,8]{2,1,0:T(2,128)S(1)} %fusion.18, f32[8,2,8,1024]{3,2,1,0:T(8,128)S(1)} %fusion.8), kind=kOutput, calls=%fused_computation.15 | convolution fusion | flops 33965184 | bytes 4751872 | tf_op jit(solution)/shard_map/skgt,sktd->skgd/dot_general | solution.py:75
  145.3 25.4 %all_gather.3 = bf16[64,2048]{1,0:T(8,128)(2,1)S(1)} all-gather(bf16[8,2048]{1,0:T(8,128)(2,1)S(1)} %bitcast.71), channel_id=1, replica_groups=mesh['dp'=8,'tensor'=4] {'dp'}, dimensions={0}, use_global_device_ids=true | all-gather | bytes 294912 | tf_op jit(solution)/shard_map/all_gather | solution.py:82
  170.7 3.0 %fusion.19 = f32[64,1024]{1,0:T(8,128)S(1)} fusion(bf16[64,2048]{1,0:T(8,128)(2,1)S(1)} %all_gather.3, bf16[2048,1024]{1,0:T(8,128)(2,1)} %param.13), kind=kOutput, calls=%fused_computation.43 | convolution fusion | flops 268435456 | bytes 4718592 | tf_op jit(solution)/shard_map/dot_general | solution.py:81
  173.7 21.2 %all-reduce.1 = bf16[64,1024]{1,0:T(8,128)(2,1)} all-reduce(f32[64,1024]{1,0:T(8,128)S(1)} %fusion.19), channel_id=1, replica_groups=mesh['dp'=8,'tensor'=4] {'tensor'}, use_global_device_ids=true, to_apply=%region_5.6 | all-reduce | flops 65536 | bytes 393216 | tf_op jit(solution)/shard_map/psum | solution.py:86
  (13 shorter events, 0.1 us)
Async XLA Ops:
  0.6 138.0 %copy-start = (bf16[8,16,128]{2,1,0:T(8,128)(2,1)S(1)}, bf16[8,16,128]{2,1,0:T(8,128)(2,1)}, u32[]{:S(2)}) copy-start(bf16[8,16,128]{2,1,0:T(8,128)(2,1)} %param.7) | copy-start | bytes 98308
  3.7 40.1 %all-to-all-start = ((bf16[8,2,1]{1,2,0:T(2,128)(2,1)}), bf16[8,2,1]{1,2,0:T(2,128)(2,1)S(1)}, u32[]{:S(2)}, u32[]{:S(2)}) async-start(bf16[8,2,1]{1,2,0:T(2,128)(2,1)} %convert_element_type.79), calls=%async_computation | async-start | bytes 8192 | tf_op jit(solution)/shard_map/all_to_all | solution.py:41
  41.8 7.3 %copy-start.1 = (s32[8,8]{1,0:T(8,128)S(1)}, s32[8,8]{1,0:T(8,128)}, u32[]{:S(2)}) copy-start(s32[8,8]{1,0:T(8,128)} %param.11) | copy-start | bytes 772
  41.8 7.4 %copy-start.2 = (s32[8]{0:T(128)S(1)}, s32[8]{0:T(128)}, u32[]{:S(2)}) copy-start(s32[8]{0:T(128)} %param.12) | copy-start | bytes 100
  43.7 52.3 %all-to-all-start.1 = ((bf16[16,2,2,128,128]{4,3,2,1,0:T(8,128)(2,1)}), bf16[16,2,2,128,128]{4,3,2,1,0:T(8,128)(2,1)S(1)}, u32[]{:S(2)}, u32[]{:S(2)}) async-start(bf16[16,2,2,128,128]{4,3,2,1,0:T(8,128)(2,1)} %bitcast.24), calls=%async_computation.1 | async-start | bytes 4194304 | tf_op jit(solution)/shard_map/all_to_all | solution.py:40
where the time goes:
time: 196 us; the launch traced here: 195 us
  local copies, waits for them, and re-layouts  67.2 us (34%)
  blocking collectives  46.6 us (24%)
  waiting for transfers between devices  46.5 us (24%)
  matrix products  18.6 us (9%)
  starting transfers between devices  11.8 us (6%)
  other arithmetic  2.78 us (1%)
    all_to_all x1, waiting for transfers between devices, body(): lax.all_to_all(outgoing, 'dp', split_axis=0, concat_axis=0, tiled=True)  46.5 us
    unnamed x14, local copies, waits for them, and re-layouts  45.6 us
    all_gather x1, blocking collectives, body(): lax.all_gather(attention, 'dp', axis=0, tiled=True)  25.4 us
    psum x1, blocking collectives, body(): summed = lax.psum(partial_sums, 'tensor')  21.2 us
    dot_general x1, matrix products, body(): jnp.dot(hit_table.astype(jnp.bfloat16), arrived.reshape(holding_rows, -1)...  10.8 us
    gather x1, local copies, waits for them, and re-layouts, body(): gathered = new_pages[block_table]  9.14 us
    gather x1, local copies, waits for them, and re-layouts, body(): picked = flat_pages[move_list[0]]  7.81 us
    all_to_all x1, starting transfers between devices, body(): lax.all_to_all(slot_tags, 'dp', split_axis=0, concat_axis=0, tiled=True)  6.37 us
  transfers between devices with their start and end apart: 2, of which 1 were waited for; matrix products, arithmetic and copies ran while one was open for 17% of the time, Pallas kernels for 0%

commit v1 on v0

--- a/solution.py
+++ b/solution.py
@@ -8,6 +8,11 @@
 BLOCK = 128
 BLOCKS = 8
 CAP = 2
+
+
+def add_all(block, mesh_axis):
+    parts = lax.all_gather(block, mesh_axis)
+    return jnp.sum(parts, axis=0)
 
 
 def body(query, kv_pages, move_plan, move_count, block_table, seq_lens, out_weight):
@@ -83,7 +88,7 @@
         out_weight,
         preferred_element_type=jnp.float32,
     )
-    summed = lax.psum(partial_sums, "tensor")
+    summed = add_all(partial_sums, "tensor")
     return (new_pages, summed.astype(jnp.bfloat16))
 
 

time: 196 us -> 214 us (1.092)
  waiting for transfers between devices: 46.5 us -> 69.8 us
  blocking collectives: 46.6 us -> 25.4 us
  between operations: 1.4 us -> 14.8 us
    all_gather x0 -> x1, waiting for transfers between devices: none -> 23.4 us  [add_all(): parts = lax.all_gather(block, mesh_axis)]
    psum x1 -> x0, blocking collectives: 21.2 us -> none  [body(): summed = lax.psum(partial_sums, 'tensor')]
  transfers between devices with their start and end apart: 2 -> 3, of which waited for: 1 -> 2; matrix products, arithmetic and copies ran while one was open for 17% -> 16% of each run, Pallas kernels for 0% -> 0%
where the time goes in v1:
time: 214 us; the launch traced here: 213 us
  waiting for transfers between devices  69.8 us (33%)
  local copies, waits for them, and re-layouts  67.2 us (31%)
  blocking collectives  25.4 us (12%)
  matrix products  19.3 us (9%)
  between operations  14.8 us (7%)
  starting transfers between devices  11.8 us (6%)
  other arithmetic  4.76 us (2%)
    all_to_all x1, waiting for transfers between devices, body(): lax.all_to_all(outgoing, 'dp', split_axis=0, concat_axis=0, tiled=True)  46.4 us
    unnamed x14, local copies, waits for them, and re-layouts  45.6 us
    all_gather x1, blocking collectives, body(): lax.all_gather(attention, 'dp', axis=0, tiled=True)  25.4 us
    all_gather x1, waiting for transfers between devices, add_all(): parts = lax.all_gather(block, mesh_axis)  23.4 us
    dot_general x1, matrix products, body(): jnp.dot(hit_table.astype(jnp.bfloat16), arrived.reshape(holding_rows, -1)...  10.8 us
    gather x1, local copies, waits for them, and re-layouts, body(): gathered = new_pages[block_table]  9.14 us
    gather x1, local copies, waits for them, and re-layouts, body(): picked = flat_pages[move_list[0]]  7.81 us
    all_to_all x1, starting transfers between devices, body(): lax.all_to_all(slot_tags, 'dp', split_axis=0, concat_axis=0, tiled=True)  6.37 us
  transfers between devices with their start and end apart: 3, of which 2 were waited for; matrix products, arithmetic and copies ran while one was open for 16% of the time, Pallas kernels for 0%

profile of v1, /device:TPU:1, one launch (start us, length us, event | category | flops | bytes accessed | tf_op | source)
XLA Modules:
  0.0 213.2 jit_solution(12264082250084426535)
XLA Ops:
  7.2 0.7 slice_bitcast_fusion
  8.5 0.2 convert_reduce_fusion
  8.7 0.7 add_select_fusion
  9.4 0.1 select_reduce_fusion
  9.5 0.7 convert_element_type.79
  10.2 6.4 %all-to-all-start = ((bf16[8,2,1]{1,2,0:T(2,128)(2,1)}), bf16[8,2,1]{1,2,0:T(2,128)(2,1)S(1)}, u32[]{:S(2)}, u32[]{:S(2)}) async-start(bf16[8,2,1]{1,2,0:T(2,128)(2,1)} %convert_element_type.79), calls=%async_computation | async-start | bytes 8192 | tf_op jit(solution)/shard_map/all_to_all | solution.py:46
  16.6 0.7 fusion.16
  17.2 8.8 %pad.2 = bf16[72,512,128]{2,1,0:T(8,128)(2,1)} pad(bf16[70,512,128]{2,1,0:T(8,128)(2,1)} %bitcast.70, bf16[]{:T(256)} %constant.38), padding=0_2x0_0x0_0 | pad | bytes 18612226
  26.0 13.8 %copy.21 = bf16[9,8,512,128]{3,1,2,0:T(8,128)(2,1)} copy(bf16[9,8,512,128]{3,2,1,0:T(8,128)(2,1)} %bitcast.63) | data formatting | bytes 18874368
  39.8 7.8 %gather_fusion = bf16[12,65536]{1,0:T(8,128)(2,1)S(1)} fusion(bf16[70,65536]{1,0:T(8,128)(2,1)} %bitcast.60, s32[1024]{0:T(1024)S(1)} %pad_clamp_fusion.1), kind=kCustom, calls=%fused_computation | custom fusion | bytes 3145776 | tf_op jit(solution)/shard_map/gather | solution.py:36
  47.7 0.7 fusion.4
  48.4 1.9 copy.22
  50.2 5.4 %all-to-all-start.1 = ((bf16[16,2,2,128,128]{4,3,2,1,0:T(8,128)(2,1)}), bf16[16,2,2,128,128]{4,3,2,1,0:T(8,128)(2,1)S(1)}, u32[]{:S(2)}, u32[]{:S(2)}) async-start(bf16[16,2,2,128,128]{4,3,2,1,0:T(8,128)(2,1)} %bitcast.25), calls=%async_computation.1 | async-start | bytes 4194304 | tf_op jit(solution)/shard_map/all_to_all | solution.py:45
  55.8 0.1 reshape.158
  55.9 0.1 iota_compare_fusion
  55.9 0.1 convert_element_type.72
  56.0 0.1 fusion.12
  56.1 46.4 %all-to-all-done.1 = bf16[16,2,2,128,128]{4,3,2,1,0:T(8,128)(2,1)S(1)} async-done(((bf16[16,2,2,128,128]{4,3,2,1,0:T(8,128)(2,1)}), bf16[16,2,2,128,128]{4,3,2,1,0:T(8,128)(2,1)S(1)}, u32[]{:S(2)}, u32[]{:S(2)}) %all-to-all-start.1) | async-done | bytes 2097184 | tf_op jit(solution)/shard_map/all_to_all | solution.py:45
  102.6 10.8 %fusion.1 = bf16[70,65536]{1,0:T(8,128)(2,1)} fusion(bf16[70,65536]{1,0:T(8,128)(2,1)} %bitcast.61, pred[70]{0:T(512)(128)(4,1)S(1)} %fusion.12, bf16[2,8,512,128]{3,2,1,0:T(8,128)(2,1)S(1)} %bitcast.71, s32[16]{0:T(128)S(1)} %convert_element_type.72), kind=kOutput, calls=%fused_computation.4 | convolution fusion | flops 155976800 | bytes 20447366 | tf_op jit(solution)/shard_map/dot_general | solution.py:50
  113.3 9.9 %copy.24 = bf16[9,8,512,128]{3,2,1,0:T(8,128)(2,1)} copy(bf16[9,8,512,128]{3,1,2,0:T(8,128)(2,1)} %bitcast.62) | data formatting | bytes 18874368
  123.3 8.4 %slice.29 = bf16[70,512,128]{2,1,0:T(8,128)(2,1)} slice(bf16[72,512,128]{2,1,0:T(8,128)(2,1)} %bitcast.64), slice={[0:70], [0:512], [0:128]} | slice | bytes 18350080
  131.6 9.1 %gather_fusion.1 = bf16[64,2,2,128,128]{4,3,2,1,0:T(8,128)(2,1)} fusion(bf16[70,2,2,128,128]{4,3,2,1,0:T(8,128)(2,1)} %bitcast.65, s32[1024]{0:T(1024)S(1)} %pad_clamp_fusion), kind=kCustom, calls=%fused_computation.1 | custom fusion | bytes 16777472 | tf_op jit(solution)/shard_map/gather | solution.py:62
  140.8 3.8 %fusion.17 = (bf16[8,8,2,1,128,128]{5,4,3,2,1,0:T(8,128)(2,1)S(1)}, bf16[8,8,2,1,128,128]{5,4,3,2,1,0:T(8,128)(2,1)S(1)}) fusion(bf16[8,8,2,2,128,128]{5,4,3,2,1,0:T(8,128)(2,1)} %bitcast.67), kind=kLoop, calls=%fused_computation.41 | loop fusion | bytes 16777216 | tf_op jit(solution)/shard_map/slice | solution.py:63
  144.6 0.6 copy.19
  145.2 1.2 fusion.8
  146.4 0.3 fusion.18
  146.6 2.2 %copy.20 = bf16[8,8,2,1,128,128]{5,4,1,2,0,3:T(8,128)(2,1)} copy(bf16[8,8,2,1,128,128]{5,4,3,2,1,0:T(8,128)(2,1)S(1)} %get-tuple-element.3) | data formatting | bytes 8388608
  148.9 2.9 %fusion.9 = bf16[1,8,16,128]{3,2,1,0:T(8,128)(2,1)S(1)} fusion(bf16[8,2,1024,128]{3,2,1,0:T(8,128)(2,1)} %bitcast.68, f32[8,2,8]{2,1,0:T(2,128)S(1)} %fusion.18, f32[8,2,8,1024]{3,2,1,0:T(8,128)S(1)} %fusion.8), kind=kOutput, calls=%fused_computation.15 | convolution fusion | flops 33965184 | bytes 4751872 | tf_op jit(solution)/shard_map/skgt,sktd->skgd/dot_general | solution.py:80
  151.8 25.4 %all_gather.9 = bf16[64,2048]{1,0:T(8,128)(2,1)S(1)} all-gather(bf16[8,2048]{1,0:T(8,128)(2,1)S(1)} %bitcast.73), channel_id=1, replica_groups=mesh['dp'=8,'tensor'=4] {'dp'}, dimensions={0}, use_global_device_ids=true | all-gather | bytes 294912 | tf_op jit(solution)/shard_map/all_gather | solution.py:87
  177.2 3.8 %fusion.19 = f32[64,1024]{1,0:T(8,128)} fusion(bf16[64,2048]{1,0:T(8,128)(2,1)S(1)} %all_gather.9, bf16[2048,1024]{1,0:T(8,128)(2,1)} %param.13), kind=kOutput, calls=%fused_computation.43 | convolution fusion | flops 268435456 | bytes 4718592 | tf_op jit(solution)/shard_map/dot_general | solution.py:86
  181.0 23.4 %all-gather.3.cloned.1.call-done = f32[256,1024]{1,0:T(8,128)} async-done(((f32[64,1024]{1,0:T(8,128)}), f32[256,1024]{1,0:T(8,128)}) %all-gather.3.cloned.1.call-update) | async-done | bytes 1048592 | tf_op jit(solution)/shard_map/all_gather | solution.py:14
  204.4 2.0 reduce_sum.39
  (16 shorter events, 0.1 us)
Async XLA Ops:
  7.2 138.0 %copy-start = (bf16[8,16,128]{2,1,0:T(8,128)(2,1)S(1)}, bf16[8,16,128]{2,1,0:T(8,128)(2,1)}, u32[]{:S(2)}) copy-start(bf16[8,16,128]{2,1,0:T(8,128)(2,1)} %param.7) | copy-start | bytes 98308
  10.2 40.1 %all-to-all-start = ((bf16[8,2,1]{1,2,0:T(2,128)(2,1)}), bf16[8,2,1]{1,2,0:T(2,128)(2,1)S(1)}, u32[]{:S(2)}, u32[]{:S(2)}) async-start(bf16[8,2,1]{1,2,0:T(2,128)(2,1)} %convert_element_type.79), calls=%async_computation | async-start | bytes 8192 | tf_op jit(solution)/shard_map/all_to_all | solution.py:46
  48.3 7.4 %copy-start.1 = (s32[8,8]{1,0:T(8,128)S(1)}, s32[8,8]{1,0:T(8,128)}, u32[]{:S(2)}) copy-start(s32[8,8]{1,0:T(8,128)} %param.11) | copy-start | bytes 772
  48.4 7.5 %copy-start.2 = (s32[8]{0:T(128)S(1)}, s32[8]{0:T(128)}, u32[]{:S(2)}) copy-start(s32[8]{0:T(128)} %param.12) | copy-start | bytes 100
  50.2 52.3 %all-to-all-start.1 = ((bf16[16,2,2,128,128]{4,3,2,1,0:T(8,128)(2,1)}), bf16[16,2,2,128,128]{4,3,2,1,0:T(8,128)(2,1)S(1)}, u32[]{:S(2)}, u32[]{:S(2)}) async-start(bf16[16,2,2,128,128]{4,3,2,1,0:T(8,128)(2,1)} %bitcast.25), calls=%async_computation.1 | async-start | bytes 4194304 | tf_op jit(solution)/shard_map/all_to_all | solution.py:45
  55.7 148.7 %all-gather.3.cloned.1.call-start = ((), (), s32[]{:S(2)}) async-start(), calls=%async_computation.2 | async-start | bytes 1310720 | tf_op jit(solution)/shard_map/all_gather | solution.py:14
Sparse Core Ops, SparseCore 0:
  181.1 23.2 all-gather.2
